TPU v7x, 128 devices: a whole 4x4x4 slice. The times are simulated.
128 devices in a mesh: dp: 8 (over x_hi, z), expert: 16 (over y, x_lo, core).
Axes of the slice: x: 4 (x_hi: 2, x_lo: 2; x = x_hi * 2 + x_lo), y: 4, z: 4, core: 2. Of those that a mesh axis runs over, the one named last changes fastest.
Arguments:
- tokens: bfloat16 [32768, 2048], P(('dp', 'expert')), may hold values from -6 to 6
- expert_ids: int32 [32768, 4], P(('dp', 'expert')), may hold values from 0 to 15, as said below
- gates: float32 [32768, 4], P(('dp', 'expert')), may hold values from 0.1 to 1
- w_gate: bfloat16 [16, 2048, 384], P('expert'), may hold values from -0.125 to 0.125
- w_up: bfloat16 [16, 2048, 384], P('expert'), may hold values from -0.125 to 0.125
- w_down: bfloat16 [16, 2048, 384], P('expert'), may hold values from -0.3125 to 0.3125
- cotangent: bfloat16 [32768, 2048], P(('dp', 'expert')), may hold values from -6 to 6
Outputs:
- mixed: bfloat16 [32768, 2048], P(('dp', 'expert'))
- tokens_grad: bfloat16 [32768, 2048], P(('dp', 'expert'))
- gates_grad: float32 [32768, 4], P(('dp', 'expert'))
- gate_grad: float32 [16, 2048, 384], P('expert', 'dp')
- up_grad: float32 [16, 2048, 384], P('expert', 'dp')
- down_grad: float32 [16, 2048, 384], P('expert', 'dp')
Inputs may be any that keep to these rules, and one draw needn't show every extreme that they name: `expert_ids`: each row holds 4 different experts. One expert, the same in every draw position, is named by every token. Among the 256 tokens of one device every other expert is named at most 52 times, and one of them is named exactly 52 times on every device.
All inputs are finite; a program needn't handle non-finite values.
Results may differ from a plain program's by a relative error of at most 0.014.
Values may be sent and summed in bfloat16 or wider, within the bound.
A program may use at most 128 MiB of HBM per device.

v0:
```python
import jax
import jax.numpy as jnp
from jax import lax
from jax.sharding import PartitionSpec as P

D = 2048
FF = 384
TOPK = 4


def broadcast(value, axis, source):
    kept = jnp.where(lax.axis_index(axis) == source, value, 0).astype(value.dtype)
    return lax.psum(kept, axis)


def expert_forward(rows, weight_gate, weight_up, weight_down):
    gate_act = jnp.dot(rows, weight_gate, preferred_element_type=jnp.float32)
    up_act = jnp.dot(rows, weight_up, preferred_element_type=jnp.float32)
    hidden = (jax.nn.silu(gate_act) * up_act).astype(jnp.bfloat16)
    output = lax.dot_general(
        hidden, weight_down, (((1,), (1,)), ((), ())), preferred_element_type=jnp.float32
    ).astype(jnp.bfloat16)
    return (gate_act, up_act, hidden, output)


def expert_backward(rows, upstream, weight_gate, weight_up, weight_down, gate_act, up_act, hidden):
    hidden_grad = jnp.dot(upstream, weight_down, preferred_element_type=jnp.float32)
    sigma = jax.nn.sigmoid(gate_act)
    gate_pre = (hidden_grad * up_act * sigma * (1.0 + gate_act * (1.0 - sigma))).astype(
        jnp.bfloat16
    )
    up_pre = (hidden_grad * gate_act * sigma).astype(jnp.bfloat16)
    contract = (((1,), (1,)), ((), ()))
    input_part = (
        lax.dot_general(gate_pre, weight_gate, contract, preferred_element_type=jnp.float32)
        + lax.dot_general(up_pre, weight_up, contract, preferred_element_type=jnp.float32)
    ).astype(jnp.bfloat16)
    over_rows = (((0,), (0,)), ((), ()))
    grad_gate = lax.dot_general(rows, gate_pre, over_rows, preferred_element_type=jnp.float32)
    grad_upper = lax.dot_general(rows, up_pre, over_rows, preferred_element_type=jnp.float32)
    grad_down = lax.dot_general(upstream, hidden, over_rows, preferred_element_type=jnp.float32)
    return (input_part, grad_gate, grad_upper, grad_down)


def per_device(tokens, expert_ids, gates, w_gate, w_up, w_down, cotangent):
    experts = lax.axis_size("expert")
    tok_rows = tokens.shape[0]
    capacity = (tok_rows * (TOPK - 1) + experts - 2) // (experts - 1)
    over_rows = (((0,), (0,)), ((), ()))
    highest = lax.Precision.HIGHEST
    expert_range = jnp.arange(experts, dtype=jnp.int32)
    matches = (expert_ids[:, :, None] == expert_range).astype(jnp.int32)
    counts = jnp.sum(matches, axis=(0, 1))
    hot_expert = jnp.argmax(counts)
    is_hot = expert_ids == hot_expert
    flat_matches = matches.reshape(tok_rows * TOPK, experts)
    before = jnp.cumsum(flat_matches, axis=0) - flat_matches
    position = jnp.sum(before * flat_matches, axis=1)
    target = jnp.where(is_hot.reshape(-1), -1, expert_ids.reshape(-1) * capacity + position)
    slot_ids = jnp.arange(experts * capacity, dtype=jnp.int32)
    dispatch_f = (slot_ids[:, None] == target[None, :]).astype(jnp.float32)
    per_token_f = jnp.sum(dispatch_f.reshape(experts * capacity, tok_rows, TOPK), axis=2)
    per_token = per_token_f.astype(jnp.bfloat16)
    slot_gate = jnp.dot(
        dispatch_f, gates.reshape(-1), precision=highest, preferred_element_type=jnp.float32
    )
    own_weights = (w_gate[0], w_up[0], w_down[0])
    shadow = (
        broadcast(own_weights[0], "expert", hot_expert),
        broadcast(own_weights[1], "expert", hot_expert),
        broadcast(own_weights[2], "expert", hot_expert),
    )
    outgoing = jnp.dot(per_token, tokens, preferred_element_type=jnp.float32).astype(jnp.bfloat16)
    outgoing = outgoing.reshape(experts, capacity, D)
    rows = lax.all_to_all(outgoing, "expert", split_axis=0, concat_axis=0, tiled=True)
    leading = rows.shape[:2]
    gate_act, up_act, hidden, output = expert_forward(rows.reshape(-1, D), *own_weights)
    received, expert_out, gate_act, up_act, hidden = (
        rows,
        output.reshape(leading + (D,)),
        gate_act.reshape(leading + (FF,)),
        up_act.reshape(leading + (FF,)),
        hidden.reshape(leading + (FF,)),
    )
    returned = lax.all_to_all(expert_out, "expert", split_axis=0, concat_axis=0, tiled=True)
    hot_gate, hot_up, hot_hidden, hot_out = expert_forward(tokens, *shadow)
    returned_f = returned.reshape(-1, D).astype(jnp.float32)
    weighted = slot_gate[:, None] * returned_f
    mixed_cold = lax.dot_general(
        per_token_f, weighted, over_rows, precision=highest, preferred_element_type=jnp.float32
    )
    hot_weight = jnp.sum(jnp.where(is_hot, gates, 0.0), axis=1)
    hot_out_f = hot_out.astype(jnp.float32)
    mixed = (mixed_cold + hot_weight[:, None] * hot_out_f).astype(jnp.bfloat16)
    upstream = cotangent.astype(jnp.float32)
    copied = jnp.dot(per_token, cotangent, preferred_element_type=jnp.float32)
    slot_dot = jnp.sum(returned_f * copied, axis=1)
    cold_gates = jnp.dot(
        slot_dot, dispatch_f, precision=highest, preferred_element_type=jnp.float32
    ).reshape(tok_rows, TOPK)
    hot_dot = jnp.sum(upstream * hot_out_f, axis=1)
    gates_grad = cold_gates + jnp.where(is_hot, hot_dot[:, None], 0.0)
    outgoing_grad = (slot_gate[:, None] * copied).astype(jnp.bfloat16)
    incoming_grad = lax.all_to_all(
        outgoing_grad.reshape(experts, capacity, D),
        "expert",
        split_axis=0,
        concat_axis=0,
        tiled=True,
    )
    input_rows, own_gate, own_upper, own_down = expert_backward(
        received.reshape(-1, D),
        incoming_grad.reshape(-1, D),
        *own_weights,
        gate_act.reshape(-1, FF),
        up_act.reshape(-1, FF),
        hidden.reshape(-1, FF)
    )
    back_rows = lax.all_to_all(
        input_rows.reshape(experts, capacity, D), "expert", split_axis=0, concat_axis=0, tiled=True
    )
    cold_input = lax.dot_general(
        per_token, back_rows.reshape(-1, D), over_rows, preferred_element_type=jnp.float32
    )
    hot_upstream = (hot_weight[:, None] * upstream).astype(jnp.bfloat16)
    hot_input, hot_gate_grad, hot_upper_grad, hot_down_grad = expert_backward(
        tokens, hot_upstream, *shadow, hot_gate, hot_up, hot_hidden
    )
    tokens_grad = (cold_input + hot_input.astype(jnp.float32)).astype(jnp.bfloat16)
    own_part = jnp.stack([own_gate, own_upper, own_down])
    hot_part = jnp.stack([hot_gate_grad, hot_upper_grad, hot_down_grad])
    is_owner = lax.axis_index("expert") == hot_expert
    hot_total = lax.psum(hot_part.astype(jnp.bfloat16), "expert").astype(jnp.float32)
    grads = lax.psum_scatter(
        own_part + jnp.where(is_owner, hot_total, 0.0), "dp", scatter_dimension=1, tiled=True
    )
    return (mixed, tokens_grad, gates_grad, grads[0][None], grads[1][None], grads[2][None])


def solution(mesh):
    return jax.shard_map(
        per_device,
        mesh=mesh,
        in_specs=(
            P(("dp", "expert"), None),
            P(("dp", "expert"), None),
            P(("dp", "expert"), None),
            P("expert", None, None),
            P("expert", None, None),
            P("expert", None, None),
            P(("dp", "expert"), None),
        ),
        out_specs=(
            P(("dp", "expert"), None),
            P(("dp", "expert"), None),
            P(("dp", "expert"), None),
            P("expert", "dp", None),
            P("expert", "dp", None),
            P("expert", "dp", None),
        ),
        check_vma=False,
    )
```

profile of v0, /device:TPU:0, one launch (start us, length us, event | category | flops | bytes accessed | tf_op | source)
XLA Modules:
  0.0 584.9 jit_solution(7026955467745829882)
XLA Ops:
  7.2 0.9 convert_reduce_fusion.1
  8.1 0.8 copy.52
  9.1 0.7 iota_reduce_fusion
  9.8 4.5 reduce-window.6
  15.0 1.4 select_reduce_fusion.1
  16.4 0.7 add_select_fusion.1
  17.1 0.5 convert_reduce_fusion
  17.6 2.8 convolution_convert_fusion.1
  20.4 4.6 reshape.98
  25.0 5.7 all-to-all-start
  31.5 2.9 bitcast_select_fusion
  34.4 2.1 bitcast_select_fusion.1
  36.6 62.9 %all-to-all-done = bf16[16,52,2048]{2,1,0:T(8,128)(2,1)} async-done(((bf16[16,52,2048]{2,1,0:T(8,128)(2,1)}), bf16[16,52,2048]{2,1,0:T(8,128)(2,1)}, u32[]{:S(2)}, u32[]{:S(2)}) %all-to-all-start) | async-done | bytes 3407904 | tf_op jit(solution)/shard_map/all_to_all | solution.py:75
  99.4 4.7 reshape.99
  104.1 4.5 fusion.28
  108.7 3.0 multiply_convert_fusion.3
  111.7 0.8 copy-done.23
  112.5 3.7 convolution_convert_fusion
  116.2 4.6 reshape.100
  120.8 5.1 all-to-all-start.1
  126.1 0.2 copy.57
  126.4 0.1 reshape.96
  126.5 1.6 fusion.30
  128.1 92.6 %all-reduce.6.cloned.1.call-done = (bf16[2048,384]{1,0:T(8,128)(2,1)}, bf16[2048,384]{1,0:T(8,128)(2,1)}, bf16[2048,384]{1,0:T(8,128)(2,1)}) async-done(((bf16[2048,384]{1,0:T(8,128)(2,1)}, bf16[2048,384]{1,0:T(8,128)(2,1)}, bf16[2048,384]{1,0:T(8,128)(2,1)}), (bf16[2048,384]{1,0:T(8,128)(2,1)}, bf16[2048,384]{1,0:T(8,128)(2,1)}, bf16[2048,384]{1,0:T(8,128)(2,1)})) %all-reduce.6.cloned.1.call-update) | async-done | bytes 4718608 | tf_op jit(solution)/shard_map/psum | solution.py:13
  220.8 2.1 convolution_bitcast_fusion.4
  222.9 0.6 convolution_bitcast_fusion.3
  223.6 0.6 copy-done.2
  224.1 0.5 copy-done.10
  224.6 1.0 multiply_convert_fusion.4
  225.6 1.9 fusion.9
  227.5 2.0 fusion.10
  229.6 5.4 reshape.105
  235.0 5.8 multiply_reduce_fusion
  240.8 4.5 reshape.101
  245.3 4.5 all-to-all-start.2
  249.9 0.8 fusion.8
  250.7 0.6 copy-done.5
  251.3 3.6 pad_maximum_fusion
  254.9 0.2 reduce-scatter.2.cloned.1.call-start
  255.1 63.2 %all-to-all-done.2 = bf16[16,52,2048]{2,1,0:T(8,128)(2,1)} async-done(((bf16[16,52,2048]{2,1,0:T(8,128)(2,1)}), bf16[16,52,2048]{2,1,0:T(8,128)(2,1)}, u32[]{:S(2)}, u32[]{:S(2)}) %all-to-all-start.2) | async-done | bytes 3407904 | tf_op jit(solution)/shard_map/all_to_all | solution.py:104
  318.4 4.6 reshape.102
  323.0 6.2 %convolution_bitcast_fusion = f32[1,2048,384]{2,1,0:T(8,128)} fusion(bf16[832,2048]{1,0:T(8,128)(2,1)} %reshape.102, bf16[832,384]{1,0:T(8,128)(2,1)S(1)} %copy-done.24), kind=kOutput, calls=%fused_computation.17 | convolution fusion | flops 1308622848 | bytes 7192576 | tf_op jit(solution)/shard_map/dot_general | solution.py:41
  329.2 2.3 multiply_convert_fusion.1
  331.5 4.0 convolution_bitcast_fusion.1
  335.5 4.0 convolution_bitcast_fusion.2
  339.5 77.1 %all-reduce.4.cloned.1.call-done = bf16[3,2048,384]{2,1,0:T(8,128)(2,1)} async-done(((bf16[3,2048,384]{2,1,0:T(8,128)(2,1)}), bf16[3,2048,384]{2,1,0:T(8,128)(2,1)}) %all-reduce.4.cloned.1.call-update) | async-done | bytes 4718608 | tf_op jit(solution)/shard_map/psum | solution.py:133
  416.6 9.4 %maximum_add_fusion = f32[3,2048,384]{2,1,0:T(8,128)} fusion(f32[1,2048,384]{2,1,0:T(8,128)} %convolution_bitcast_fusion, f32[1,2048,384]{2,1,0:T(8,128)} %convolution_bitcast_fusion.1, f32[1,2048,384]{2,1,0:T(8,128)} %convolution_bitcast_fusion.2, bf16[3,2048,384]{2,1,0:T(8,128)(2,1)} %all-reduce.4.cloned.1.call-done, pred[]{:T(512)S(6)} %eq.93), kind=kLoop, calls=%fused_computation | loop fusion | flops 11796480 | bytes 23592960 | tf_op jit(solution)/shard_map/add | solution.py:135
  426.0 3.5 fusion.26
  429.5 3.7 add_convert_fusion
  433.2 4.7 reshape.103
  437.9 4.5 all-to-all-start.3
  442.4 0.8 copy.61
  443.2 2.9 fusion.18
  446.2 0.7 fusion.43
  446.9 0.7 copy-done.14
  447.6 2.2 fusion.16
  449.8 1.7 select_reduce_fusion
  451.6 0.6 select_add_fusion
  452.2 10.3 %fusion.11 = bf16[256,2048]{1,0:T(8,128)(2,1)} fusion(f32[832,256]{1,0:T(8,128)S(1)} %convert_reduce_fusion, f32[832,2048]{1,0:T(8,128)} %reshape.105, f32[832]{0:T(1024)S(1)} %fusion.30, bf16[256,2048]{1,0:T(8,128)(2,1)S(1)} %get-tuple-element.38, f32[256]{0:T(256)S(1)} %get-tuple-element.23), kind=kOutput, calls=%fused_computation.32 | convolution fusion | flops 5238292480 | bytes 9769216 | tf_op jit(solution)/shard_map/dot_general | solution.py:89
  462.5 46.8 %all-to-all-done.3 = bf16[16,52,2048]{2,1,0:T(8,128)(2,1)} async-done(((bf16[16,52,2048]{2,1,0:T(8,128)(2,1)}), bf16[16,52,2048]{2,1,0:T(8,128)(2,1)}, u32[]{:S(2)}, u32[]{:S(2)}) %all-to-all-start.3) | async-done | bytes 3407904 | tf_op jit(solution)/shard_map/all_to_all | solution.py:119
  509.2 4.6 reshape.104
  513.8 4.9 fusion.14
  518.7 57.2 %reduce-scatter.2.cloned.1.call-done = f32[3,256,384]{2,1,0:T(8,128)} async-done(((f32[3,2048,384]{2,1,0:T(8,128)}), f32[3,256,384]{2,1,0:T(8,128)}) %reduce-scatter.2.cloned.1.call-update) | async-done | bytes 1179664 | tf_op jit(solution)/shard_map/reduce_scatter | solution.py:134
  575.9 2.3 fusion.42
  (73 shorter events, 1.5 us)
Async XLA Ops:
  7.2 10.4 %copy-start = (bf16[256,2048]{1,0:T(8,128)(2,1)S(1)}, bf16[256,2048]{1,0:T(8,128)(2,1)}, u32[]{:S(2)}) copy-start(bf16[256,2048]{1,0:T(8,128)(2,1)} %param.7) | copy-start | bytes 3145732
  16.4 109.7 %copy-start.20 = (pred[256,4]{0,1:T(4,128)(4,1)}, pred[256,4]{0,1:T(4,128)(4,1)S(1)}, u32[]{:S(2)}) copy-start(pred[256,4]{0,1:T(4,128)(4,1)S(1)} %get-tuple-element.24) | copy-start | bytes 3076
  25.0 74.5 %all-to-all-start = ((bf16[16,52,2048]{2,1,0:T(8,128)(2,1)}), bf16[16,52,2048]{2,1,0:T(8,128)(2,1)}, u32[]{:S(2)}, u32[]{:S(2)}) async-start(bf16[16,52,2048]{2,1,0:T(8,128)(2,1)} %reshape.98), calls=%async_computation | async-start | bytes 7340032 | tf_op jit(solution)/shard_map/all_to_all | solution.py:75
  30.6 3.8 copy-start.3
  30.7 190.1 %all-reduce.6.cloned.1.call-start = ((), (), s32[]{:S(2)}) async-start(), calls=%async_computation.7 | async-start | bytes 9437184 | tf_op jit(solution)/shard_map/psum | solution.py:13
  31.5 2.9 copy-start.6
  104.1 4.5 copy-start.7
  108.7 3.0 copy-start.25
  108.7 3.9 copy-start.11
  111.7 0.8 copy-start.23
  120.8 5.1 copy-start.19
  120.8 108.8 %all-to-all-start.1 = ((bf16[16,52,2048]{2,1,0:T(8,128)(2,1)}), bf16[16,52,2048]{2,1,0:T(8,128)(2,1)}, u32[]{:S(2)}, u32[]{:S(2)}) async-start(bf16[16,52,2048]{2,1,0:T(8,128)(2,1)} %reshape.100), calls=%async_computation.1 | async-start | bytes 7340032 | tf_op jit(solution)/shard_map/all_to_all | solution.py:85
  220.8 2.2 copy-start.13
  222.9 1.2 copy-start.2
  222.9 1.7 copy-start.10
  245.3 73.1 %all-to-all-start.2 = ((bf16[16,52,2048]{2,1,0:T(8,128)(2,1)}), bf16[16,52,2048]{2,1,0:T(8,128)(2,1)}, u32[]{:S(2)}, u32[]{:S(2)}) async-start(bf16[16,52,2048]{2,1,0:T(8,128)(2,1)} %reshape.101), calls=%async_computation.2 | async-start | bytes 7340032 | tf_op jit(solution)/shard_map/all_to_all | solution.py:104
  249.8 166.7 %all-reduce.4.cloned.1.call-start = ((), (), s32[]{:S(2)}) async-start(), calls=%async_computation.5 | async-start | bytes 9437184 | tf_op jit(solution)/shard_map/psum | solution.py:133
  249.9 1.4 copy-start.5
  254.9 68.1 %copy-start.24 = (bf16[832,384]{1,0:T(8,128)(2,1)S(1)}, bf16[832,384]{1,0:T(8,128)(2,1)}, u32[]{:S(2)}) copy-start(bf16[832,384]{1,0:T(8,128)(2,1)} %copy-done.23) | copy-start | bytes 1916932
  254.9 321.0 %reduce-scatter.2.cloned.1.call-start = ((), (), s32[]{:S(2)}) async-start(), calls=%async_computation.6 | async-start | bytes 10616832 | tf_op jit(solution)/shard_map/reduce_scatter | solution.py:134
  322.9 6.2 %copy-start.9 = (bf16[832,2048]{1,0:T(8,128)(2,1)S(1)}, bf16[832,2048]{1,0:T(8,128)(2,1)}, u32[]{:S(2)}) copy-start(bf16[832,2048]{1,0:T(8,128)(2,1)} %reshape.102) | copy-start | bytes 10223620
  322.9 6.2 %copy-start.12 = (bf16[1,2048,384]{2,1,0:T(8,128)(2,1)S(1)}, bf16[1,2048,384]{2,1,0:T(8,128)(2,1)}, u32[]{:S(2)}) copy-start(bf16[1,2048,384]{2,1,0:T(8,128)(2,1)} %param.12) | copy-start | bytes 4718596
  322.9 6.2 %copy-start.26 = (f32[832,384]{1,0:T(8,128)S(1)}, f32[832,384]{1,0:T(8,128)}, u32[]{:S(2)}) copy-start(f32[832,384]{1,0:T(8,128)} %copy-done.25) | copy-start | bytes 3833860
  323.0 6.2 %copy-start.27 = (f32[832,384]{1,0:T(8,128)S(1)}, f32[832,384]{1,0:T(8,128)}, u32[]{:S(2)}) copy-start(f32[832,384]{1,0:T(8,128)} %get-tuple-element.36) | copy-start | bytes 3833860
  329.1 2.3 copy-start.8
  331.4 4.0 copy-start.16
  426.0 3.5 copy-start.4
  426.0 3.5 copy-start.17
  437.9 71.3 %all-to-all-start.3 = ((bf16[16,52,2048]{2,1,0:T(8,128)(2,1)}), bf16[16,52,2048]{2,1,0:T(8,128)(2,1)}, u32[]{:S(2)}, u32[]{:S(2)}) async-start(bf16[16,52,2048]{2,1,0:T(8,128)(2,1)} %reshape.103), calls=%async_computation.3 | async-start | bytes 7340032 | tf_op jit(solution)/shard_map/all_to_all | solution.py:119
  443.2 2.9 copy-start.15
  446.2 1.4 copy-start.14
  447.6 2.2 copy-start.18
  447.6 4.0 copy-start.21
  447.6 4.0 copy-start.22
  513.8 64.4 %copy-start.1 = (bf16[256,2048]{1,0:T(8,128)(2,1)S(1)}, bf16[256,2048]{1,0:T(8,128)(2,1)}, u32[]{:S(2)}) copy-start(bf16[256,2048]{1,0:T(8,128)(2,1)} %param.7) | copy-start | bytes 3145732
Sparse Core Ops, SparseCore 0:
  36.7 184.0 all-reduce.5
  255.0 161.5 all-reduce.3
  426.1 149.7 reduce-scatter.1
where the time goes:
time: 592 us; the launch traced here: 585 us
  waiting for transfers between devices  400 us (68%)
  matrix products  74.5 us (13%)
  local copies, waits for them, and re-layouts  46.2 us (8%)
  other arithmetic  29.2 us (5%)
  starting transfers between devices  20.1 us (3%)
  between operations  15.1 us (3%)
    psum x1, waiting for transfers between devices, broadcast(): return lax.psum(kept, axis)  92.6 us
    psum x1, waiting for transfers between devices, per_device(): lax.psum(hot_part.astype(jnp.bfloat16), 'expert').astype(jnp.float32)  77.1 us
    all_to_all x1, waiting for transfers between devices, per_device(): lax.all_to_all(outgoing_grad.reshape(experts, capacity, D), 'expert', spl...  63.2 us
    all_to_all x1, waiting for transfers between devices, per_device(): lax.all_to_all(outgoing, 'expert', split_axis=0, concat_axis=0, tiled=True)  62.9 us
    reduce_scatter x1, waiting for transfers between devices, per_device(): lax.psum_scatter(own_part + jnp.where(is_owner, hot_total, 0.0), 'dp', sc...  57.2 us
    all_to_all x1, waiting for transfers between devices, per_device(): lax.all_to_all(input_rows.reshape(experts, capacity, D), 'expert', split_...  46.8 us
  transfers between devices with their start and end apart: 7, of which 6 were waited for; matrix products, arithmetic and copies ran while one was open for 17% of the time, Pallas kernels for 0%

commit v1 on v0

--- a/solution.py
+++ b/solution.py
@@ -130,7 +130,11 @@
     own_part = jnp.stack([own_gate, own_upper, own_down])
     hot_part = jnp.stack([hot_gate_grad, hot_upper_grad, hot_down_grad])
     is_owner = lax.axis_index("expert") == hot_expert
-    hot_total = lax.psum(hot_part.astype(jnp.bfloat16), "expert").astype(jnp.float32)
+    hot_total = (
+        jax.lax.all_gather(hot_part.astype(jnp.bfloat16), axis_name="expert")
+        .sum(axis=0)
+        .astype(jnp.float32)
+    )
     grads = lax.psum_scatter(
         own_part + jnp.where(is_owner, hot_total, 0.0), "dp", scatter_dimension=1, tiled=True
     )

time: 592 us -> 864 us (1.46)
  blocking collectives: 0 us -> 178 us
  waiting for transfers between devices: 400 us -> 476 us
  other arithmetic: 29.2 us -> 52.9 us
  starting transfers between devices: 20.1 us -> 10.7 us
    all_to_all x0 -> x2, blocking collectives: none -> 178 us  [the longest x1 89.3 us: per_device(): lax.all_to_all(outgoing, 'expert', split_axis=0, concat_axis=0, tiled=True)]
    all_gather x0 -> x1, waiting for transfers between devices: none -> 147 us  [per_device(): jax.lax.all_gather(hot_part.astype(jnp.bfloat16), axis_name='expert')]
    all_to_all x2 -> x0, waiting for transfers between devices: 126 us -> none  [the longest x1 63.2 us: per_device(): lax.all_to_all(outgoing_grad.reshape(experts, capacity, D), 'expert', spl...]
    all_to_all x1, waiting for transfers between devices: 0.01 us -> 82 us  [per_device(): lax.all_to_all(expert_out, 'expert', split_axis=0, concat_axis=0, tiled=T...]
    psum x1 -> x0, waiting for transfers between devices: 77.1 us -> none  [per_device(): lax.psum(hot_part.astype(jnp.bfloat16), 'expert').astype(jnp.float32)]
    psum x1, waiting for transfers between devices: 92.6 us -> 141 us  [broadcast(): return lax.psum(kept, axis)]
    reduce_sum x0 -> x1, other arithmetic: none -> 26.4 us  [per_device(): hot_total = jax.lax.all_gather(hot_part.astype(jnp.bfloat16), axis_name='...]
    all_to_all x2 -> x0, starting transfers between devices: 10.2 us -> none  [the longest x1 5.66 us: per_device(): lax.all_to_all(outgoing, 'expert', split_axis=0, concat_axis=0, tiled=True)]
  transfers between devices with their start and end apart: 7 -> 5, of which waited for: 6 -> 5; matrix products, arithmetic and copies ran while one was open for 17% -> 13% of each run, Pallas kernels for 0% -> 0%
where the time goes in v1:
time: 864 us; the launch traced here: 856 us
  waiting for transfers between devices  476 us (55%)
  blocking collectives  178 us (21%)
  matrix products  71.8 us (8%)
  other arithmetic  52.9 us (6%)
  local copies, waits for them, and re-layouts  52 us (6%)
  between operations  15 us (2%)
  starting transfers between devices  10.7 us (1%)
    all_gather x1, waiting for transfers between devices, per_device(): jax.lax.all_gather(hot_part.astype(jnp.bfloat16), axis_name='expert')  147 us
    psum x1, waiting for transfers between devices, broadcast(): return lax.psum(kept, axis)  141 us
    all_to_all x1, blocking collectives, per_device(): lax.all_to_all(outgoing, 'expert', split_axis=0, concat_axis=0, tiled=True)  89.3 us
    all_to_all x1, blocking collectives, per_device(): lax.all_to_all(outgoing_grad.reshape(experts, capacity, D), 'expert', spl...  89 us
    all_to_all x1, waiting for transfers between devices, per_device(): lax.all_to_all(expert_out, 'expert', split_axis=0, concat_axis=0, tiled=T...  82 us
    reduce_scatter x1, waiting for transfers between devices, per_device(): lax.psum_scatter(own_part + jnp.where(is_owner, hot_total, 0.0), 'dp', sc...  59 us
    all_to_all x1, waiting for transfers between devices, per_device(): lax.all_to_all(input_rows.reshape(experts, capacity, D), 'expert', split_...  47 us
    reduce_sum x1, other arithmetic, per_device(): hot_total = jax.lax.all_gather(hot_part.astype(jnp.bfloat16), axis_name='...  26.4 us
  transfers between devices with their start and end apart: 5, of which 5 were waited for; matrix products, arithmetic and copies ran while one was open for 13% of the time, Pallas kernels for 0%

profile of v1, /device:TPU:0, one launch (start us, length us, event | category | flops | bytes accessed | tf_op | source)
XLA Modules:
  0.0 856.5 jit_solution(15552599443730830953)
XLA Ops:
  7.2 1.0 convert_reduce_fusion.1
  8.2 0.7 iota_reduce_fusion
  9.5 2.8 bitcast_select_fusion
  12.4 2.0 bitcast_select_fusion.1
  14.5 0.6 copy-done.19
  15.1 0.7 select_reduce_fusion.1
  15.8 141.1 %all-reduce.3.cloned.1.call-done = (bf16[2048,384]{1,0:T(8,128)(2,1)}, bf16[2048,384]{1,0:T(8,128)(2,1)}, bf16[2048,384]{1,0:T(8,128)(2,1)}) async-done(((bf16[2048,384]{1,0:T(8,128)(2,1)}, bf16[2048,384]{1,0:T(8,128)(2,1)}, bf16[2048,384]{1,0:T(8,128)(2,1)}), (bf16[2048,384]{1,0:T(8,128)(2,1)}, bf16[2048,384]{1,0:T(8,128)(2,1)}, bf16[2048,384]{1,0:T(8,128)(2,1)})) %all-reduce.3.cloned.1.call-update) | async-done | bytes 4718608 | tf_op jit(solution)/shard_map/psum | solution.py:13
  156.9 2.1 convolution_bitcast_fusion.3
  159.0 0.6 convolution_bitcast_fusion.4
  159.7 0.6 copy-done.2
  160.2 0.5 copy-done.10
  160.7 1.0 multiply_convert_fusion.4
  161.7 0.6 fusion.9
  162.3 0.6 fusion.8
  162.9 0.7 fusion.10
  163.6 2.4 pad_maximum_fusion
  166.0 6.6 copy.80
  172.6 0.1 copy.69
  173.0 4.5 reduce-window.6
  177.6 0.1 copy.71
  178.2 0.5 convert_reduce_fusion
  178.8 2.9 convolution_convert_fusion.1
  181.6 5.1 reshape.146
  186.8 89.3 %all_to_all.20 = bf16[16,52,2048]{2,1,0:T(8,128)(2,1)} all-to-all(bf16[16,52,2048]{2,1,0:T(8,128)(2,1)} %reshape.146), channel_id=1, replica_groups=mesh['dp'=8,'expert'=16] {'expert'}, dimensions={0} | all-to-all | bytes 6815744 | tf_op jit(solution)/shard_map/all_to_all | solution.py:75
  276.0 4.7 reshape.147
  280.7 4.5 fusion.28
  285.2 3.0 multiply_convert_fusion.3
  288.3 3.8 convolution_convert_fusion
  292.0 4.6 reshape.148
  296.6 4.6 all-to-all-start.1
  301.4 0.2 copy.74
  301.6 0.1 copy.75
  301.7 0.1 reshape.144
  302.0 1.6 fusion.30
  303.6 82.0 %all-to-all-done.1 = bf16[16,52,2048]{2,1,0:T(8,128)(2,1)} async-done(((bf16[16,52,2048]{2,1,0:T(8,128)(2,1)}), bf16[16,52,2048]{2,1,0:T(8,128)(2,1)}, u32[]{:S(2)}, u32[]{:S(2)}) %all-to-all-start.1) | async-done | bytes 3407904 | tf_op jit(solution)/shard_map/all_to_all | solution.py:85
  385.6 5.4 reshape.153
  391.0 5.9 multiply_reduce_fusion
  396.9 4.5 reshape.149
  401.5 89.0 %all_to_all.21 = bf16[16,52,2048]{2,1,0:T(8,128)(2,1)} all-to-all(bf16[16,52,2048]{2,1,0:T(8,128)(2,1)} %reshape.149), channel_id=1, replica_groups=mesh['dp'=8,'expert'=16] {'expert'}, dimensions={0} | all-to-all | bytes 6815744 | tf_op jit(solution)/shard_map/all_to_all | solution.py:104
  490.5 4.6 reshape.150
  495.1 6.1 convolution_bitcast_fusion
  501.3 2.3 multiply_convert_fusion.1
  503.6 4.0 convolution_bitcast_fusion.1
  507.6 4.0 convolution_bitcast_fusion.2
  511.6 146.8 %all-gather.2.cloned.1.call-done = bf16[16,3,2048,384]{3,2,1,0:T(8,128)(2,1)} async-done(((bf16[1,3,2048,384]{3,2,1,0:T(8,128)(2,1)}), bf16[16,3,2048,384]{3,2,1,0:T(8,128)(2,1)}) %all-gather.2.cloned.1.call-update) | async-done | bytes 75497488 | tf_op jit(solution)/shard_map/all_gather | solution.py:134
  658.4 26.4 %reduce_sum.75 = bf16[3,2048,384]{2,1,0:T(8,128)(2,1)} reduce(bf16[16,3,2048,384]{3,2,1,0:T(8,128)(2,1)} %all-gather.2.cloned.1.call-done, bf16[]{:T(256)} %constant.30.clone.1), dimensions={0}, to_apply=%region_12.13 | reduce | flops 35389440 | bytes 80216064 | tf_op jit(solution)/shard_map/reduce_sum | solution.py:135
  684.8 9.4 %maximum_add_fusion = f32[3,2048,384]{2,1,0:T(8,128)} fusion(f32[1,2048,384]{2,1,0:T(8,128)} %convolution_bitcast_fusion, f32[1,2048,384]{2,1,0:T(8,128)} %convolution_bitcast_fusion.1, f32[1,2048,384]{2,1,0:T(8,128)} %convolution_bitcast_fusion.2, bf16[3,2048,384]{2,1,0:T(8,128)(2,1)} %reduce_sum.75, pred[]{:T(512)S(6)} %eq.93), kind=kLoop, calls=%fused_computation | loop fusion | flops 11796480 | bytes 23592960 | tf_op jit(solution)/shard_map/add | solution.py:139
  694.2 3.5 fusion.26
  697.8 3.7 add_convert_fusion
  701.4 4.6 reshape.151
  706.1 5.9 all-to-all-start.3
  712.0 0.8 copy.78
  712.8 2.9 fusion.18
  715.7 0.7 fusion.43
  716.5 0.7 copy-done.13
  717.2 2.1 fusion.16
  719.3 1.7 select_reduce_fusion
  721.1 0.6 select_add_fusion
  721.7 10.3 %fusion.11 = bf16[256,2048]{1,0:T(8,128)(2,1)} fusion(f32[832,256]{1,0:T(8,128)S(1)} %convert_reduce_fusion, f32[832,2048]{1,0:T(8,128)} %reshape.153, f32[832]{0:T(1024)S(1)} %fusion.30, bf16[256,2048]{1,0:T(8,128)(2,1)S(1)} %get-tuple-element.44, f32[256]{0:T(256)S(1)} %get-tuple-element.29), kind=kOutput, calls=%fused_computation.32 | convolution fusion | flops 5238292480 | bytes 9769216 | tf_op jit(solution)/shard_map/dot_general | solution.py:89
  731.9 47.0 %all-to-all-done.3 = bf16[16,52,2048]{2,1,0:T(8,128)(2,1)} async-done(((bf16[16,52,2048]{2,1,0:T(8,128)(2,1)}), bf16[16,52,2048]{2,1,0:T(8,128)(2,1)}, u32[]{:S(2)}, u32[]{:S(2)}) %all-to-all-start.3) | async-done | bytes 3407904 | tf_op jit(solution)/shard_map/all_to_all | solution.py:119
  778.9 4.6 reshape.152
  783.5 4.9 fusion.14
  788.5 59.0 %reduce-scatter.2.cloned.1.call-done = f32[3,256,384]{2,1,0:T(8,128)} async-done(((f32[3,2048,384]{2,1,0:T(8,128)}), f32[3,256,384]{2,1,0:T(8,128)}) %reduce-scatter.2.cloned.1.call-update) | async-done | bytes 1179664 | tf_op jit(solution)/shard_map/reduce_scatter | solution.py:138
  847.5 2.3 fusion.42
  (75 shorter events, 1.3 us)
Async XLA Ops:
  7.2 149.7 %copy-start = (bf16[256,2048]{1,0:T(8,128)(2,1)S(1)}, bf16[256,2048]{1,0:T(8,128)(2,1)}, u32[]{:S(2)}) copy-start(bf16[256,2048]{1,0:T(8,128)(2,1)} %param.7) | copy-start | bytes 3145732
  7.2 5.2 copy-start.3
  7.2 149.7 %all-reduce.3.cloned.1.call-start = ((), (), s32[]{:S(2)}) async-start(), calls=%async_computation.7 | async-start | bytes 9437184 | tf_op jit(solution)/shard_map/psum | solution.py:13
  9.5 2.8 copy-start.6
  14.4 0.7 copy-start.19
  14.4 0.7 copy-start.20
  14.4 644.0 %all-gather.2.cloned.1.call-start = ((), (), s32[]{:S(2)}) async-start(), calls=%async_computation.5 | async-start | bytes 80216064 | tf_op jit(solution)/shard_map/all_gather | solution.py:134
  15.8 162.5 %copy-start.22 = (pred[256,4]{0,1:T(4,128)(4,1)}, pred[256,4]{0,1:T(4,128)(4,1)S(1)}, u32[]{:S(2)}) copy-start(pred[256,4]{0,1:T(4,128)(4,1)S(1)} %get-tuple-element.30) | copy-start | bytes 3076
  156.8 2.2 copy-start.14
  159.0 1.2 copy-start.2
  159.0 1.7 copy-start.10
  280.7 4.5 copy-start.4
  280.7 4.5 copy-start.7
  285.2 3.0 copy-start.26
  285.2 3.0 copy-start.11
  296.6 4.7 copy-start.23
  296.6 4.9 copy-start.21
  296.6 89.0 %all-to-all-start.1 = ((bf16[16,52,2048]{2,1,0:T(8,128)(2,1)}), bf16[16,52,2048]{2,1,0:T(8,128)(2,1)}, u32[]{:S(2)}, u32[]{:S(2)}) async-start(bf16[16,52,2048]{2,1,0:T(8,128)(2,1)} %reshape.148), calls=%async_computation.1 | async-start | bytes 7340032 | tf_op jit(solution)/shard_map/all_to_all | solution.py:85
  301.3 546.2 %reduce-scatter.2.cloned.1.call-start = ((), (), s32[]{:S(2)}) async-start(), calls=%async_computation.6 | async-start | bytes 10616832 | tf_op jit(solution)/shard_map/reduce_scatter | solution.py:138
  495.1 6.2 copy-start.9
  495.1 6.2 copy-start.12
  495.1 6.2 copy-start.27
  495.1 6.2 copy-start.28
  501.3 2.3 copy-start.8
  503.6 4.0 copy-start.16
  694.2 3.5 copy-start.5
  694.2 3.5 copy-start.17
  706.1 72.8 %all-to-all-start.3 = ((bf16[16,52,2048]{2,1,0:T(8,128)(2,1)}), bf16[16,52,2048]{2,1,0:T(8,128)(2,1)}, u32[]{:S(2)}, u32[]{:S(2)}) async-start(bf16[16,52,2048]{2,1,0:T(8,128)(2,1)} %reshape.151), calls=%async_computation.3 | async-start | bytes 7340032 | tf_op jit(solution)/shard_map/all_to_all | solution.py:119
  712.8 2.9 copy-start.15
  715.7 1.4 copy-start.13
  717.1 2.1 copy-start.18
  717.1 3.9 copy-start.24
  717.1 3.9 copy-start.25
  783.5 66.2 %copy-start.1 = (bf16[256,2048]{1,0:T(8,128)(2,1)S(1)}, bf16[256,2048]{1,0:T(8,128)(2,1)}, u32[]{:S(2)}) copy-start(bf16[256,2048]{1,0:T(8,128)(2,1)} %param.7) | copy-start | bytes 3145732
Sparse Core Ops, SparseCore 0:
  14.5 142.2 all-reduce.2
  172.8 485.5 all-gather.1
  694.3 153.0 reduce-scatter.1
